TPU v7x, 256 devices: a whole 4x4x8 slice. The times are simulated.
256 devices in a mesh: dp: 32 (over x, z_hi, core), expert: 8 (over y, z_lo).
Axes of the slice: x: 4, y: 4, z: 8 (z_hi: 4, z_lo: 2; z = z_hi * 2 + z_lo), core: 2. Of those that a mesh axis runs over, the one named last changes fastest.
Arguments:
- tokens: bfloat16 [73728, 2048], P(('dp', 'expert')), may hold values from -24 to 24
- expert_ids: int32 [73728, 8], P(('dp', 'expert')), may hold values from 0 to 127, all different within a row
- gates: float32 [73728, 8], P(('dp', 'expert')), may hold values from 0.05 to 1
- cotangent: bfloat16 [73728, 2048], P(('dp', 'expert')), may hold values from -1.25 to 1.25
- gate_weight: bfloat16 [8, 2048, 768], P('expert'), may hold values from -0.125 to 0.125
- up_weight: bfloat16 [8, 2048, 768], P('expert'), may hold values from -0.125 to 0.125
- down_weight: bfloat16 [8, 2048, 768], P('expert'), may hold values from -0.21875 to 0.21875
- block_masks: int32 [8, 3, 16, 6], P('expert'), may hold values 0 or 1
Outputs:
- combined: bfloat16 [73728, 2048], P(('dp', 'expert'))
- grad_gate: float32 [8, 2048, 768], P('expert', 'dp')
- grad_up: float32 [8, 2048, 768], P('expert', 'dp')
- grad_down: float32 [8, 2048, 768], P('expert', 'dp')
Inputs may be any that keep to these rules, and one draw needn't show every extreme that they name: `expert_ids`: each row names 8 different experts.
All inputs are finite; a program needn't handle non-finite values. No bound on the sum of `block_masks` on one device may be relied on, other than what follows from the above.
Results may differ from a plain program's by a relative error of at most 0.014.
Values may be sent and summed in bfloat16 or wider, within the bound.
A program may use at most 128 MiB of HBM per device.

v0:
```python
import jax
import jax.numpy as jnp
from jax import lax
from jax.sharding import PartitionSpec as P

TILE = 128
MICRO = 2
CAP = 18


def expand_masks(block_masks):
    count, three, row_blocks, col_blocks = block_masks.shape
    spread = jnp.broadcast_to(
        block_masks.astype(jnp.bfloat16)[:, :, :, None, :, None],
        (count, three, row_blocks, TILE, col_blocks, TILE),
    )
    return spread.reshape(count, three, row_blocks * TILE, col_blocks * TILE)


def route(ids, gates, experts):
    onehot = (ids[:, :, None] == jnp.arange(experts, dtype=jnp.int32)).astype(jnp.int32)
    flat = onehot.reshape(-1, experts)
    before = jnp.cumsum(flat, axis=0) - flat
    slot_index = jnp.sum(before * flat, axis=1)
    which = jnp.sum(flat * jnp.arange(experts, dtype=jnp.int32), axis=1)
    live = (jnp.sum(flat, axis=1) > 0) & (slot_index < CAP)
    where_to = jnp.where(live, which * CAP + slot_index, -1).reshape(ids.shape)
    select = where_to[:, :, None] == jnp.arange(experts * CAP, dtype=jnp.int32)
    sends = jnp.sum(select.astype(jnp.float32), axis=1).astype(jnp.bfloat16)
    rounded = gates.astype(jnp.bfloat16).astype(jnp.float32)
    weights = jnp.sum(jnp.where(select, rounded[:, :, None], 0.0), axis=1).astype(jnp.bfloat16)
    return (sends, weights)


def body(tokens, expert_ids, gates, cotangent, gate_weight, up_weight, down_weight, block_masks):
    n_expert = lax.axis_size("expert")
    local = gate_weight.shape[0]
    experts = local * n_expert
    width = tokens.shape[1]
    tok_mb = tokens.shape[0] // MICRO
    rows = n_expert * CAP
    masks = expand_masks(block_masks)
    w_gate = gate_weight * masks[:, 0]
    w_up = up_weight * masks[:, 1]
    w_down = down_weight * masks[:, 2]
    outputs = []
    saved_x = []
    saved_dy = []
    saved_hidden = []
    saved_dgate = []
    saved_dup = []
    for micro in range(MICRO):
        first = micro * tok_mb
        x_part = tokens[first : first + tok_mb]
        sends, weights = route(
            expert_ids[first : first + tok_mb], gates[first : first + tok_mb], experts
        )
        x_buf = jnp.einsum("tc,td->cd", sends, x_part, preferred_element_type=jnp.float32).astype(
            jnp.bfloat16
        )
        x_buf = x_buf.reshape(n_expert, local, CAP, width)
        dy_buf = jnp.einsum(
            "tc,td->cd",
            weights,
            cotangent[first : first + tok_mb],
            preferred_element_type=jnp.float32,
        ).astype(jnp.bfloat16)
        dy_buf = dy_buf.reshape(n_expert, local, CAP, width)
        x_rows = lax.all_to_all(x_buf, "expert", split_axis=0, concat_axis=2, tiled=True)
        x_rows = x_rows.reshape(local, rows, width)
        gate_pre = jnp.einsum("erd,edf->erf", x_rows, w_gate, preferred_element_type=jnp.float32)
        up_pre = jnp.einsum("erd,edf->erf", x_rows, w_up, preferred_element_type=jnp.float32)
        hidden = (jax.nn.silu(gate_pre) * up_pre).astype(jnp.bfloat16)
        result = jnp.einsum(
            "erf,edf->erd", hidden, w_down, preferred_element_type=jnp.float32
        ).astype(jnp.bfloat16)
        returned = lax.all_to_all(
            result.reshape(1, local, rows, width), "expert", split_axis=2, concat_axis=0, tiled=True
        )
        mixed = jnp.dot(
            weights, returned.reshape(experts * CAP, width), preferred_element_type=jnp.float32
        )
        outputs.append(mixed.astype(jnp.bfloat16))
        dy_rows = lax.all_to_all(dy_buf, "expert", split_axis=0, concat_axis=2, tiled=True)
        dy_rows = dy_rows.reshape(local, rows, width)
        d_hidden = jnp.einsum("erd,edf->erf", dy_rows, w_down, preferred_element_type=jnp.float32)
        sig = jax.nn.sigmoid(gate_pre)
        d_gate = (d_hidden * up_pre * sig * (1.0 + gate_pre * (1.0 - sig))).astype(jnp.bfloat16)
        d_up = (d_hidden * gate_pre * sig).astype(jnp.bfloat16)
        saved_x.append(x_rows)
        saved_dy.append(dy_rows)
        saved_hidden.append(hidden)
        saved_dgate.append(d_gate)
        saved_dup.append(d_up)
    x_all = jnp.concatenate(saved_x, axis=1)
    dy_all = jnp.concatenate(saved_dy, axis=1)
    hidden_all = jnp.concatenate(saved_hidden, axis=1)
    dgate_all = jnp.concatenate(saved_dgate, axis=1)
    dup_all = jnp.concatenate(saved_dup, axis=1)
    g_gate = (
        jnp.einsum("erd,erf->edf", x_all, dgate_all, preferred_element_type=jnp.float32)
        * masks[:, 0]
    )
    g_up = (
        jnp.einsum("erd,erf->edf", x_all, dup_all, preferred_element_type=jnp.float32) * masks[:, 1]
    )
    g_down = (
        jnp.einsum("erd,erf->edf", dy_all, hidden_all, preferred_element_type=jnp.float32)
        * masks[:, 2]
    )
    grad_gate, grad_up, grad_down = (
        lax.psum_scatter(g_gate.astype(jnp.bfloat16), "dp", scatter_dimension=1, tiled=True).astype(
            jnp.float32
        ),
        lax.psum_scatter(g_up.astype(jnp.bfloat16), "dp", scatter_dimension=1, tiled=True).astype(
            jnp.float32
        ),
        lax.psum_scatter(g_down.astype(jnp.bfloat16), "dp", scatter_dimension=1, tiled=True).astype(
            jnp.float32
        ),
    )
    return (jnp.concatenate(outputs, axis=0), grad_gate, grad_up, grad_down)


def solution(mesh):
    return jax.shard_map(
        body,
        mesh=mesh,
        in_specs=(
            P(("dp", "expert"), None),
            P(("dp", "expert"), None),
            P(("dp", "expert"), None),
            P(("dp", "expert"), None),
            P("expert", None, None),
            P("expert", None, None),
            P("expert", None, None),
            P("expert", None, None, None),
        ),
        out_specs=(
            P(("dp", "expert"), None),
            P("expert", "dp", None),
            P("expert", "dp", None),
            P("expert", "dp", None),
        ),
        check_vma=False,
    )
```

profile of v0, /device:TPU:1, one launch (start us, length us, event | category | flops | bytes accessed | tf_op | source)
XLA Modules:
  0.0 437.3 jit_solution(4560271060682134590)
XLA Ops:
  8.4 2.3 reduce-window.14
  15.5 6.4 %all-to-all-start = ((bf16[8,1,18,2048]{3,2,1,0:T(8,128)(2,1)}), bf16[8,1,18,2048]{3,2,1,0:T(8,128)(2,1)}, u32[]{:S(2)}, u32[]{:S(2)}) async-start(bf16[8,1,18,2048]{3,2,1,0:T(8,128)(2,1)} %bitcast.1), calls=%async_computation | async-start | bytes 1572864 | tf_op jit(solution)/shard_map/all_to_all | solution.py:69
  21.9 4.9 %broadcast_in_dim.47 = bf16[3,16,128,6,128]{2,1,4,3,0:T(8,128)(2,1)} broadcast(bf16[3,16,6]{1,2,0:T(8,128)(2,1)S(1)} %bitcast.170), dimensions={0,1,3} | broadcast | bytes 9437760 | tf_op jit(solution)/shard_map/broadcast_in_dim | solution.py:13
  26.9 14.9 %broadcast_in_dim.48 = bf16[1,3,2048,768]{2,3,1,0:T(8,128)(2,1)} reshape(bf16[3,16,128,6,128]{2,1,4,3,0:T(8,128)(2,1)} %broadcast_in_dim.47) | data formatting | bytes 18874368 | tf_op jit(solution)/shard_map/broadcast_in_dim | solution.py:13
  41.7 6.1 %fusion.69 = (bf16[1,1,2048,768]{2,3,1,0:T(8,128)(2,1)}, bf16[1,1,2048,768]{2,3,1,0:T(8,128)(2,1)S(1)}, bf16[1,1,2048,768]{2,3,1,0:T(8,128)(2,1)}) fusion(bf16[1,3,2048,768]{2,3,1,0:T(8,128)(2,1)} %broadcast_in_dim.48), kind=kLoop, calls=%fused_computation.114 | loop fusion | bytes 18874368 | tf_op jit(solution)/shard_map/slice | solution.py:45
  49.3 2.9 copy.73
  52.2 3.2 copy.72
  57.5 4.7 %copy.74 = bf16[1,1,2048,768]{3,2,1,0:T(8,128)(2,1)} copy(bf16[1,1,2048,768]{2,3,1,0:T(8,128)(2,1)} %get-tuple-element.14) | data formatting | bytes 6291456
  62.3 2.3 reduce-window.16
  65.4 5.1 %all-to-all-start.4 = ((bf16[8,1,18,2048]{3,2,1,0:T(8,128)(2,1)}), bf16[8,1,18,2048]{3,2,1,0:T(8,128)(2,1)}, u32[]{:S(2)}, u32[]{:S(2)}) async-start(bf16[8,1,18,2048]{3,2,1,0:T(8,128)(2,1)} %bitcast.163), calls=%async_computation.4 | async-start | bytes 1572864 | tf_op jit(solution)/shard_map/all_to_all | solution.py:84
  71.3 2.2 convolution_convert_fusion.3
  75.7 4.8 %bitcast_multiply_fusion = bf16[1,2048,768]{2,1,0:T(8,128)(2,1)} fusion(bf16[1,2048,768]{2,1,0:T(8,128)(2,1)} %param.14, bf16[1,1,2048,768]{3,2,1,0:T(8,128)(2,1)} %copy.74), kind=kLoop, calls=%fused_computation.14 | loop fusion | flops 1572864 | bytes 9437184 | tf_op jit(solution)/shard_map/mul | solution.py:45
  82.1 4.2 all-to-all-start.2
  86.3 2.2 convolution_convert_fusion
  95.0 4.8 %fusion.13 = f32[144,768]{1,0:T(8,128)} fusion(bf16[144,2048]{1,0:T(8,128)(2,1)} %reshape.298, bf16[1,2048,768]{2,1,0:T(8,128)(2,1)} %param.13, bf16[1,1,2048,768]{3,2,1,0:T(8,128)(2,1)} %copy.73), kind=kOutput, calls=%fused_computation.17 | convolution fusion | flops 454557696 | bytes 7323648 | tf_op jit(solution)/shard_map/erd,edf->erf/dot_general | solution.py:72
  101.4 5.0 %all-to-all-start.5 = ((bf16[8,1,18,2048]{3,2,1,0:T(8,128)(2,1)}), bf16[8,1,18,2048]{3,2,1,0:T(8,128)(2,1)}, u32[]{:S(2)}, u32[]{:S(2)}) async-start(bf16[8,1,18,2048]{3,2,1,0:T(8,128)(2,1)} %bitcast.164), calls=%async_computation.5 | async-start | bytes 1572864 | tf_op jit(solution)/shard_map/all_to_all | solution.py:84
  106.7 3.8 fusion.50
  112.7 4.8 %fusion.11 = f32[144,768]{1,0:T(8,128)} fusion(bf16[144,2048]{1,0:T(8,128)(2,1)} %reshape.306, bf16[1,2048,768]{2,1,0:T(8,128)(2,1)} %param.13, bf16[1,1,2048,768]{3,2,1,0:T(8,128)(2,1)} %copy.73), kind=kOutput, calls=%fused_computation.15 | convolution fusion | flops 454557696 | bytes 7323648 | tf_op jit(solution)/shard_map/erd,edf->erf/dot_general | solution.py:72
  121.3 3.8 fusion.51
  129.3 5.9 %fusion.21 = bf16[1,2048,768]{2,1,0:T(8,128)(2,1)} fusion(bf16[1,1,2048,768]{3,2,1,0:T(8,128)(2,1)} %copy.74, bf16[1,144,2048]{2,1,0:T(8,128)(2,1)} %reshape.319, bf16[1,144,2048]{2,1,0:T(8,128)(2,1)} %reshape.318, bf16[1,144,768]{2,1,0:T(8,128)(2,1)} %bitcast.169, bf16[1,144,768]{2,1,0:T(8,128)(2,1)S(1)} %bitcast.168), kind=kOutput, calls=%fused_computation.27 | convolution fusion | flops 913932288 | bytes 7913472 | tf_op jit(solution)/shard_map/erd,erf->edf/dot_general | solution.py:108
  139.6 5.9 %fusion.20 = bf16[1,2048,768]{2,1,0:T(8,128)(2,1)} fusion(bf16[1,1,2048,768]{3,2,1,0:T(8,128)(2,1)} %copy.73, bf16[1,144,2048]{2,1,0:T(8,128)(2,1)} %reshape.310, bf16[1,144,2048]{2,1,0:T(8,128)(2,1)} %reshape.309, bf16[1,144,768]{2,1,0:T(8,128)(2,1)} %get-tuple-element.20, bf16[1,144,768]{2,1,0:T(8,128)(2,1)} %get-tuple-element.17), kind=kOutput, calls=%fused_computation.26 | convolution fusion | flops 913932288 | bytes 7913472 | tf_op jit(solution)/shard_map/erd,erf->edf/dot_general | solution.py:105
  145.8 4.8 %fusion.19 = bf16[1,2048,768]{2,1,0:T(8,128)(2,1)} fusion(bf16[1,1,2048,768]{3,2,1,0:T(8,128)(2,1)S(1)} %copy.72, bf16[1,144,2048]{2,1,0:T(8,128)(2,1)} %reshape.310, bf16[1,144,2048]{2,1,0:T(8,128)(2,1)} %reshape.309, bf16[1,144,768]{2,1,0:T(8,128)(2,1)} %get-tuple-element.21, bf16[1,144,768]{2,1,0:T(8,128)(2,1)} %get-tuple-element.18), kind=kOutput, calls=%fused_computation.25 | convolution fusion | flops 913932288 | bytes 7913472 | tf_op jit(solution)/shard_map/erd,erf->edf/dot_general | solution.py:101
  156.1 6.0 %reduce.5 = bf16[144,2048]{1,0:T(8,128)(2,1)} reduce(bf16[144,1,1,2048]{3,2,1,0:T(2,128)(2,1)} %bitcast.161, bf16[]{:T(256)} %broadcast.108), dimensions={1,2}, to_apply=%bitcast.158.reduce_sub_computation | reduce | bytes 1179650
  162.1 2.5 reshape.329
  164.6 4.9 %all-to-all-start.1 = ((bf16[8,2,18432]{2,1,0:T(2,128)(2,1)}), bf16[8,2,18432]{2,1,0:T(2,128)(2,1)}, u32[]{:S(2)}, u32[]{:S(2)}) async-start(bf16[8,2,18432]{2,1,0:T(2,128)(2,1)} %reshape.329), calls=%async_computation.1 | async-start | bytes 1179648 | tf_op jit(solution)/shard_map/all_to_all | solution.py:77
  171.7 4.1 reduce.4
  177.6 4.7 %all-to-all-start.3 = ((bf16[8,2,18432]{2,1,0:T(2,128)(2,1)}), bf16[8,2,18432]{2,1,0:T(2,128)(2,1)S(1)}, u32[]{:S(2)}, u32[]{:S(2)}) async-start(bf16[8,2,18432]{2,1,0:T(2,128)(2,1)} %reshape.327), calls=%async_computation.3 | async-start | bytes 1179648 | tf_op jit(solution)/shard_map/all_to_all | solution.py:77
  182.3 2.3 reshape.330
  184.6 5.6 %all-to-all-done.3 = bf16[8,2,18432]{2,1,0:T(2,128)(2,1)S(1)} async-done(((bf16[8,2,18432]{2,1,0:T(2,128)(2,1)}), bf16[8,2,18432]{2,1,0:T(2,128)(2,1)S(1)}, u32[]{:S(2)}, u32[]{:S(2)}) %all-to-all-start.3) | async-done | bytes 589856 | tf_op jit(solution)/shard_map/all_to_all | solution.py:77
  193.0 41.2 %reduce-scatter.8.cloned.1.call-done = bf16[1,64,768]{2,1,0:T(8,128)(2,1)} async-done(((bf16[1,2048,768]{2,1,0:T(8,128)(2,1)}), bf16[1,64,768]{2,1,0:T(8,128)(2,1)}) %reduce-scatter.8.cloned.1.call-update) | async-done | bytes 98320 | tf_op jit(solution)/shard_map/reduce_scatter | solution.py:118
  235.8 95.9 %reduce-scatter.6.cloned.1.call-done = bf16[1,64,768]{2,1,0:T(8,128)(2,1)} async-done(((bf16[1,2048,768]{2,1,0:T(8,128)(2,1)}), bf16[1,64,768]{2,1,0:T(8,128)(2,1)}) %reduce-scatter.6.cloned.1.call-update) | async-done | bytes 98320 | tf_op jit(solution)/shard_map/reduce_scatter | solution.py:115
  333.2 96.0 %reduce-scatter.4.cloned.1.call-done = bf16[1,64,768]{2,1,0:T(8,128)(2,1)} async-done(((bf16[1,2048,768]{2,1,0:T(8,128)(2,1)}), bf16[1,64,768]{2,1,0:T(8,128)(2,1)}) %reduce-scatter.4.cloned.1.call-update) | async-done | bytes 98320 | tf_op jit(solution)/shard_map/reduce_scatter | solution.py:112
  (85 shorter events, 54.9 us)
Async XLA Ops:
  7.2 14.7 %copy-start.7 = (s32[1,3,16,6]{2,0,3,1:T(1,128)S(1)}, s32[1,3,16,6]{2,0,3,1:T(1,128)}, u32[]{:S(2)}) copy-start(s32[1,3,16,6]{2,0,3,1:T(1,128)} %param.15) | copy-start | bytes 3460
  15.5 49.8 %all-to-all-start = ((bf16[8,1,18,2048]{3,2,1,0:T(8,128)(2,1)}), bf16[8,1,18,2048]{3,2,1,0:T(8,128)(2,1)}, u32[]{:S(2)}, u32[]{:S(2)}) async-start(bf16[8,1,18,2048]{3,2,1,0:T(8,128)(2,1)} %bitcast.1), calls=%async_computation | async-start | bytes 1572864 | tf_op jit(solution)/shard_map/all_to_all | solution.py:69
  41.7 6.1 %copy-start.5 = (bf16[288,2048]{1,0:T(8,128)(2,1)S(1)}, bf16[288,2048]{1,0:T(8,128)(2,1)}, u32[]{:S(2)}) copy-start(bf16[288,2048]{1,0:T(8,128)(2,1)} %param.11) | copy-start | bytes 3538948
  65.4 16.7 %all-to-all-start.4 = ((bf16[8,1,18,2048]{3,2,1,0:T(8,128)(2,1)}), bf16[8,1,18,2048]{3,2,1,0:T(8,128)(2,1)}, u32[]{:S(2)}, u32[]{:S(2)}) async-start(bf16[8,1,18,2048]{3,2,1,0:T(8,128)(2,1)} %bitcast.163), calls=%async_computation.4 | async-start | bytes 1572864 | tf_op jit(solution)/shard_map/all_to_all | solution.py:84
  82.1 19.3 %all-to-all-start.2 = ((bf16[8,1,18,2048]{3,2,1,0:T(8,128)(2,1)}), bf16[8,1,18,2048]{3,2,1,0:T(8,128)(2,1)}, u32[]{:S(2)}, u32[]{:S(2)}) async-start(bf16[8,1,18,2048]{3,2,1,0:T(8,128)(2,1)} %bitcast.165), calls=%async_computation.2 | async-start | bytes 1572864 | tf_op jit(solution)/shard_map/all_to_all | solution.py:69
  95.0 4.8 %copy-start.1 = (bf16[1,2048,768]{2,1,0:T(8,128)(2,1)S(1)}, bf16[1,2048,768]{2,1,0:T(8,128)(2,1)}, u32[]{:S(2)}) copy-start(bf16[1,2048,768]{2,1,0:T(8,128)(2,1)} %param.12) | copy-start | bytes 9437188
  95.0 4.8 %copy-start.3 = (bf16[144,2048]{1,0:T(8,128)(2,1)S(1)}, bf16[144,2048]{1,0:T(8,128)(2,1)}, u32[]{:S(2)}) copy-start(bf16[144,2048]{1,0:T(8,128)(2,1)} %reshape.298) | copy-start | bytes 1769476
  101.4 17.7 %all-to-all-start.5 = ((bf16[8,1,18,2048]{3,2,1,0:T(8,128)(2,1)}), bf16[8,1,18,2048]{3,2,1,0:T(8,128)(2,1)}, u32[]{:S(2)}, u32[]{:S(2)}) async-start(bf16[8,1,18,2048]{3,2,1,0:T(8,128)(2,1)} %bitcast.164), calls=%async_computation.5 | async-start | bytes 1572864 | tf_op jit(solution)/shard_map/all_to_all | solution.py:84
  106.5 127.7 %reduce-scatter.8.cloned.1.call-start = ((), (), s32[]{:S(2)}) async-start(), calls=%async_computation.11 | async-start | bytes 3244032 | tf_op jit(solution)/shard_map/reduce_scatter | solution.py:118
  112.7 4.8 %copy-start.2 = (bf16[1,2048,768]{2,1,0:T(8,128)(2,1)S(1)}, bf16[1,2048,768]{2,1,0:T(8,128)(2,1)}, u32[]{:S(2)}) copy-start(bf16[1,2048,768]{2,1,0:T(8,128)(2,1)} %param.12) | copy-start | bytes 9437188
  112.7 4.8 %copy-start.4 = (bf16[144,2048]{1,0:T(8,128)(2,1)S(1)}, bf16[144,2048]{1,0:T(8,128)(2,1)}, u32[]{:S(2)}) copy-start(bf16[144,2048]{1,0:T(8,128)(2,1)} %reshape.306) | copy-start | bytes 1769476
  135.2 196.4 %reduce-scatter.6.cloned.1.call-start = ((), (), s32[]{:S(2)}) async-start(), calls=%async_computation.10 | async-start | bytes 3244032 | tf_op jit(solution)/shard_map/reduce_scatter | solution.py:115
  145.5 283.7 %reduce-scatter.4.cloned.1.call-start = ((), (), s32[]{:S(2)}) async-start(), calls=%async_computation.9 | async-start | bytes 3244032 | tf_op jit(solution)/shard_map/reduce_scatter | solution.py:112
  150.6 1.9 copy-start
  153.7 15.9 %copy-start.6 = (bf16[144,768]{1,0:T(8,128)(2,1)S(1)}, bf16[144,768]{1,0:T(8,128)(2,1)}, u32[]{:S(2)}) copy-start(bf16[144,768]{1,0:T(8,128)(2,1)} %get-tuple-element.22) | copy-start | bytes 663556
  164.6 12.9 %all-to-all-start.1 = ((bf16[8,2,18432]{2,1,0:T(2,128)(2,1)}), bf16[8,2,18432]{2,1,0:T(2,128)(2,1)}, u32[]{:S(2)}, u32[]{:S(2)}) async-start(bf16[8,2,18432]{2,1,0:T(2,128)(2,1)} %reshape.329), calls=%async_computation.1 | async-start | bytes 1179648 | tf_op jit(solution)/shard_map/all_to_all | solution.py:77
  177.6 12.6 %all-to-all-start.3 = ((bf16[8,2,18432]{2,1,0:T(2,128)(2,1)}), bf16[8,2,18432]{2,1,0:T(2,128)(2,1)S(1)}, u32[]{:S(2)}, u32[]{:S(2)}) async-start(bf16[8,2,18432]{2,1,0:T(2,128)(2,1)} %reshape.327), calls=%async_computation.3 | async-start | bytes 1179648 | tf_op jit(solution)/shard_map/all_to_all | solution.py:77
Sparse Core Ops, SparseCore 0:
  135.4 98.7 reduce-scatter.7
  238.1 93.4 reduce-scatter.5
  335.6 93.5 reduce-scatter.3
where the time goes:
time: 441 us; the launch traced here: 437 us
  waiting for transfers between devices  241 us (55%)
  local copies, waits for them, and re-layouts  75.6 us (17%)
  matrix products  47.6 us (11%)
  starting transfers between devices  31 us (7%)
  other arithmetic  28.4 us (6%)
  between operations  14 us (3%)
    reduce_scatter x1, waiting for transfers between devices, body(): lax.psum_scatter(g_gate.astype(jnp.bfloat16), 'dp', scatter_dimension=1,...  96 us
    reduce_scatter x1, waiting for transfers between devices, body(): lax.psum_scatter(g_up.astype(jnp.bfloat16), 'dp', scatter_dimension=1, ti...  95.9 us
    reduce_scatter x1, waiting for transfers between devices, body(): lax.psum_scatter(g_down.astype(jnp.bfloat16), 'dp', scatter_dimension=1,...  41.2 us
    unnamed x25, local copies, waits for them, and re-layouts  19.9 us
    broadcast_in_dim x2, local copies, waits for them, and re-layouts, expand_masks(): jnp.broadcast_to(block_masks.astype(jnp.bfloat16)[:, :, :, None, :, None]...  19.8 us
    all_to_all x2, starting transfers between devices, body(): lax.all_to_all(x_buf, 'expert', split_axis=0, concat_axis=2, tiled=True)  10.6 us
    unnamed x4, other arithmetic  10.3 us
    all_to_all x2, starting transfers between devices, body(): lax.all_to_all(dy_buf, 'expert', split_axis=0, concat_axis=2, tiled=True)  10.2 us
  transfers between devices with their start and end apart: 9, of which 6 were waited for; matrix products, arithmetic and copies ran while one was open for 28% of the time, Pallas kernels for 0%

commit v1 on v0

v1 whole, which is shorter than its diff:
```python
import functools

import jax
import jax.numpy as jnp
from jax import lax
from jax.experimental import pallas as pl
from jax.experimental.pallas import tpu as pltpu
from jax.sharding import PartitionSpec as P

MESH = pl.DeviceIdType.MESH
BF = jnp.bfloat16
F32 = jnp.float32
CAP = 18
E = 8
T = 288
TM = 144
D = 2048
FF = 768
BLK = 128
NB = 18
ROWS = 16
BUCKETS = (12, 13, 14, 18)


def nn(a, b):
    return jnp.dot(a, b, preferred_element_type=F32)


def nt(a, b):
    return lax.dot_general(a, b, (((1,), (1,)), ((), ())), preferred_element_type=F32)


def iota(shape, dim):
    return lax.broadcasted_iota(jnp.int32, shape, dim)


def flag(cond):
    return jnp.where(cond, 1.0, 0.0).astype(BF)


def act_kernel(
    tok_h, ids_ref, gat_ref, cot_h, wg_h, wu_h, wd_h, msk_ref,
    xt_h, yt_h, act_h, rm_h, rr_h, wt_h, tbl_ref, cnt_ref,
    tok, cot, wg, wu, wd, sel, wsel, xs, xsr, ys, ysr, xr, xrr, yr, yrr,
    rem, g, u, acts, rm, rr, xt, yt, wt, mx, cbuf, crec,
    lsem, osem, ssem, rsem,
):
    dp = lax.axis_index("dp")
    me = lax.axis_index("expert")

    loads = [
        pltpu.make_async_copy(tok_h, tok, lsem.at[0]),
        pltpu.make_async_copy(cot_h, cot, lsem.at[1]),
        pltpu.make_async_copy(wg_h, wg, lsem.at[2]),
        pltpu.make_async_copy(wu_h, wu, lsem.at[3]),
        pltpu.make_async_copy(wd_h, wd, lsem.at[4]),
    ]
    for load in loads:
        load.start()

    barrier = pltpu.get_barrier_semaphore()
    for k in range(1, E):
        pl.semaphore_signal(
            barrier, inc=1, device_id=(dp, lax.rem(me + k, E)), device_id_type=MESH
        )

    eye8 = flag(iota((E, E), 0) == iota((E, E), 1))
    ids_t = nt(eye8, ids_ref[...].astype(F32).astype(BF))
    gat_t = nt(eye8, gat_ref[...].astype(BF))
    sub = iota((E, T), 0)
    hit = jnp.zeros((E, T), F32)
    gw = jnp.zeros((E, T), F32)
    for e in range(E):
        same = ids_t == float(e)
        hit = jnp.where(
            sub == e, jnp.sum(jnp.where(same, 1.0, 0.0), axis=0, keepdims=True), hit
        )
        gw = jnp.where(
            sub == e, jnp.sum(jnp.where(same, gat_t, 0.0), axis=0, keepdims=True), gw
        )
    t0 = iota((T, T), 0)
    t1 = iota((T, T), 1)
    earlier = flag((t0 < t1) & ((t0 < TM) == (t1 < TM)))
    before = nn(hit.astype(BF), earlier)
    lane = iota((E, T), 1)
    kept = (hit > 0.0) & (before < float(CAP))
    slot = jnp.where(kept, before + jnp.where(lane < TM, 0.0, float(CAP)), -1.0)
    row8 = iota((T, E), 0)
    owner = jnp.where(row8 < 256, row8 // 32, (row8 - 256) // 4)
    spread = flag(owner == iota((T, E), 1))
    slot_rows = nn(spread, slot.astype(BF))
    gw_rows = nn(spread, gw.astype(BF))
    want = jnp.where(t0 < 256, t0 % 32, 32 + (t0 - 256) % 4).astype(F32)
    chosen = slot_rows == want
    sel[...] = flag(chosen)
    wsel[...] = jnp.where(chosen, gw_rows, 0.0).astype(BF)

    def dispatch(matrix, source, main, tail):
        def step(n, carry):
            cols = pl.ds(pl.multiple_of(n * 512, 512), 512)
            v = nn(matrix[...], source[:, cols])
            main[:, cols] = v[:256].astype(BF)
            for e in range(E):
                tail[e, :, cols] = v[256 + 4 * e : 260 + 4 * e].astype(BF)
            return carry

        lax.fori_loop(0, 4, step, 0)

    def moves(main, tail, main_to, tail_to, kind):
        out = []
        for k in range(1, E):
            to = lax.rem(me + k, E)
            out.append(
                pltpu.make_async_remote_copy(
                    src_ref=main.at[pl.ds(pl.multiple_of(to * 32, 32), 32)],
                    dst_ref=main_to.at[pl.ds(pl.multiple_of(me * 32, 32), 32)],
                    send_sem=ssem.at[kind, k],
                    recv_sem=rsem.at[kind, k],
                    device_id=(dp, to),
                    device_id_type=MESH,
                )
            )
            out.append(
                pltpu.make_async_remote_copy(
                    src_ref=tail.at[to],
                    dst_ref=tail_to.at[me],
                    send_sem=ssem.at[kind + 1, k],
                    recv_sem=rsem.at[kind + 1, k],
                    device_id=(dp, to),
                    device_id_type=MESH,
                )
            )
        own = [
            pltpu.make_async_copy(
                main.at[pl.ds(pl.multiple_of(me * 32, 32), 32)],
                main_to.at[pl.ds(pl.multiple_of(me * 32, 32), 32)],
                lsem.at[5 + kind],
            ),
            pltpu.make_async_copy(tail.at[me], tail_to.at[me], lsem.at[6 + kind]),
        ]
        return out, own

    def merge(main_to, tail_to):
        for e in range(E):
            rem[4 * e : 4 * e + 4, :] = tail_to[e].astype(F32)
        main_to[256:288, :] = rem[...].astype(BF)

    loads[0].wait()
    dispatch(sel, tok, xs, xsr)
    pl.semaphore_wait(barrier, E - 1)
    x_moves, x_own = moves(xs, xsr, xr, xrr, 0)
    for move in x_moves + x_own:
        move.start()
    loads[1].wait()
    dispatch(wsel, cot, ys, ysr)
    y_moves, y_own = moves(ys, ysr, yr, yrr, 2)
    for move in y_moves + y_own:
        move.start()

    widths = (ROWS, BLK)
    m2 = jnp.zeros(widths, F32)
    for mat in range(3):
        put = flag(iota((6, BLK), 1) == iota((6, BLK), 0) + 6 * mat)
        m2 = m2 + nn(msk_ref[mat].astype(F32).astype(BF), put)
    tri = flag(iota((BLK, BLK), 0) <= iota((BLK, BLK), 1))
    upto = nn(m2.astype(BF), tri)
    pos = upto - 1.0
    most = jnp.max(jnp.max(upto, axis=1, keepdims=True), axis=0, keepdims=True)
    cbuf[...] = jnp.broadcast_to(most, (8, BLK))
    order = jnp.zeros(widths, F32)
    cell = iota(widths, 1).astype(F32)
    for i in range(NB):
        here = (pos[:, i : i + 1] == cell) & (m2[:, i : i + 1] > 0.0)
        order = order + jnp.where(here, float(i), 0.0)
    tbl_ref[0:16, :] = order.astype(jnp.int32)
    tbl_ref[16:32, :] = jnp.maximum(pos, 0.0).astype(jnp.int32)
    tbl_ref[32:48, :] = m2.astype(jnp.int32)
    c_moves = []
    for k in range(1, E):
        to = lax.rem(me + k, E)
        c_moves.append(
            pltpu.make_async_remote_copy(
                src_ref=cbuf,
                dst_ref=crec.at[k],
                send_sem=ssem.at[4, k],
                recv_sem=rsem.at[4, k],
                device_id=(dp, to),
                device_id_type=MESH,
            )
        )
    for move in c_moves:
        move.start()

    lift = flag(iota((6, FF), 1) // BLK == iota((6, FF), 0))
    for mat in range(3):
        mx[16 * mat : 16 * mat + 16, :] = nn(msk_ref[mat].astype(F32).astype(BF), lift)
    for load in loads[2:]:
        load.wait()

    def prune(r, carry):
        rows = pl.ds(pl.multiple_of(r * BLK, BLK), BLK)
        for mat, w in enumerate((wg, wu, wd)):
            w[rows, :] = w[rows, :] * mx[pl.ds(16 * mat + r, 1), :].astype(BF)
        return carry

    lax.fori_loop(0, ROWS, prune, 0)
    eye = flag(iota((T, T), 0) == iota((T, T), 1))
    wt[...] = nt(eye, wsel[...]).astype(BF)

    def turn(source, target):
        def step(r, carry):
            cols = pl.ds(pl.multiple_of(r * BLK, BLK), BLK)
            eye_b = flag(iota((BLK, BLK), 0) == iota((BLK, BLK), 1))
            target[r] = nt(eye_b, source[:, cols]).astype(BF)
            return carry

        lax.fori_loop(0, ROWS, step, 0)

    outs = [
        pltpu.make_async_copy(xt, xt_h, osem.at[0]),
        pltpu.make_async_copy(yt, yt_h, osem.at[1]),
        pltpu.make_async_copy(acts, act_h, osem.at[2]),
        pltpu.make_async_copy(rm, rm_h, osem.at[3]),
        pltpu.make_async_copy(rr, rr_h, osem.at[4]),
        pltpu.make_async_copy(wt, wt_h, osem.at[5]),
    ]
    outs[5].start()

    for move in x_own:
        move.wait()
    for move in x_moves:
        move.wait_recv()
    merge(xr, xrr)

    def forward(n, carry):
        cols = pl.ds(pl.multiple_of(n * 256, 256), 256)
        gv = nn(xr[...], wg[:, cols])
        uv = nn(xr[...], wu[:, cols])
        g[:, cols] = gv
        u[:, cols] = uv
        h_cols = pl.ds(pl.multiple_of(2 * FF + n * 256, 256), 256)
        acts[:, h_cols] = (gv * jax.nn.sigmoid(gv) * uv).astype(BF)
        return carry

    lax.fori_loop(0, 3, forward, 0)

    def project(n, carry):
        cols = pl.ds(pl.multiple_of(n * 256, 256), 256)
        v = nt(acts[:, 2 * FF : 3 * FF], wd[cols, :])
        rm[:, cols] = v[:256].astype(BF)
        for e in range(E):
            rr[e, :, cols] = v[256 + 4 * e : 260 + 4 * e].astype(BF)
        return carry

    lax.fori_loop(0, 8, project, 0)
    outs[3].start()
    outs[4].start()
    turn(xr, xt)
    outs[0].start()

    for move in y_own:
        move.wait()
    for move in y_moves:
        move.wait_recv()
    merge(yr, yrr)

    def backward(n, carry):
        cols = pl.ds(pl.multiple_of(n * 256, 256), 256)
        dh = nn(yr[...], wd[:, cols])
        gv = g[:, cols]
        s = jax.nn.sigmoid(gv)
        ds = dh * s
        acts[:, cols] = (ds * u[:, cols] * (1.0 + gv * (1.0 - s))).astype(BF)
        u_cols = pl.ds(pl.multiple_of(FF + n * 256, 256), 256)
        acts[:, u_cols] = (ds * gv).astype(BF)
        return carry

    lax.fori_loop(0, 3, backward, 0)
    outs[2].start()
    turn(yr, yt)
    outs[1].start()

    for move in c_moves:
        move.wait_recv()
    top = cbuf[...]
    for k in range(1, E):
        top = jnp.maximum(top, crec[k])
    cnt_ref[...] = top
    for move in x_moves + y_moves + c_moves:
        move.wait_send()
    for out in outs:
        out.wait()


def grad_kernel(
    cz,
    xt_h, yt_h, act_h, rm_h, rr_h, wt_h, tbl,
    com_h, gg_ref, gu_ref, gd_ref,
    xt, yt, acts, wt, ret, rer, rem, com, blk,
    cs, cr, sm, ra, rb, fp, fm, zz, za, zb, gp, gm,
    lsem, tsem, ssem, rsem, csem, crsem, xsem, xrsem, zsem, zrsem,
):
    na = cz // 2
    nb = cz - na
    dp = lax.axis_index("dp")
    me = lax.axis_index("expert")
    x = dp // 8
    z = (dp // 2) % 4
    c = dp % 2

    def at(xx, zz_, cc):
        return ((xx * 4 + zz_) * 2 + cc, me)

    twin = at(x, z, 1 - c)
    xp = at((x + 1) % 4, z, c)
    xm = at((x + 3) % 4, z, c)
    zp = at(x, (z + 1) % 4, c)
    zm = at(x, (z + 3) % 4, c)

    def x_of(i):
        return (x + (2, 1, 3, 0)[i]) % 4

    def z_of(t):
        step = jnp.where(t == 0, 2, jnp.where(t == 1, 1, jnp.where(t == 2, 3, 0)))
        return (z + step) % 4

    barrier = pltpu.get_barrier_semaphore()
    for peer in (twin, xp, xm, zp, zm):
        pl.semaphore_signal(barrier, inc=1, device_id=peer, device_id_type=MESH)
    for k in range(1, E):
        pl.semaphore_signal(
            barrier, inc=1, device_id=(dp, lax.rem(me + k, E)), device_id_type=MESH
        )

    loads = [
        pltpu.make_async_copy(act_h, acts, lsem.at[0]),
        pltpu.make_async_copy(wt_h, wt, lsem.at[1]),
        pltpu.make_async_copy(
            rm_h.at[pl.ds(pl.multiple_of(me * 32, 32), 32)],
            ret.at[pl.ds(pl.multiple_of(me * 32, 32), 32)],
            lsem.at[2],
        ),
        pltpu.make_async_copy(rr_h.at[me], rer.at[me], lsem.at[3]),
    ]
    loads[0].start()

    def tile_loads(t, i):
        r = x_of(i) * 4 + z_of(t)
        s = t * 4 + i
        return [
            pltpu.make_async_copy(xt_h.at[r], xt.at[s], tsem.at[0, s]),
            pltpu.make_async_copy(yt_h.at[r], yt.at[s], tsem.at[1, s]),
        ]

    for t in range(4):
        for i in range(4):
            for load in tile_loads(t, i):
                load.start()
    for load in loads[1:]:
        load.start()

    pl.semaphore_wait(barrier, 12)

    r_moves = []
    for k in range(1, E):
        to = lax.rem(me + k, E)
        r_moves.append(
            pltpu.make_async_remote_copy(
                src_ref=rm_h.at[pl.ds(pl.multiple_of(to * 32, 32), 32)],
                dst_ref=ret.at[pl.ds(pl.multiple_of(me * 32, 32), 32)],
                send_sem=ssem.at[0, k],
                recv_sem=rsem.at[0, k],
                device_id=(dp, to),
                device_id_type=MESH,
            )
        )
        r_moves.append(
            pltpu.make_async_remote_copy(
                src_ref=rr_h.at[to],
                dst_ref=rer.at[me],
                send_sem=ssem.at[1, k],
                recv_sem=rsem.at[1, k],
                device_id=(dp, to),
                device_id_type=MESH,
            )
        )
    for move in r_moves:
        move.start()

    def core_move(t, i):
        s = t * 4 + i
        return pltpu.make_async_remote_copy(
            src_ref=cs.at[s], dst_ref=cr.at[s],
            send_sem=csem.at[s], recv_sem=crsem.at[s],
            device_id=twin, device_id_type=MESH,
        )

    def x_move(kind, t):
        src, dst, peer = (
            lambda: (sm.at[4 * t, pl.ds(0, na)], ra.at[t], xp),
            lambda: (sm.at[4 * t, pl.ds(na, nb)], rb.at[t], xm),
            lambda: (sm.at[4 * t + 1, pl.ds(na, nb)], fp.at[t, pl.ds(na, nb)], xp),
            lambda: (sm.at[4 * t + 2, pl.ds(0, na)], fm.at[t, pl.ds(0, na)], xm),
            lambda: (sm.at[4 * t + 1, pl.ds(0, na)], fp.at[t, pl.ds(0, na)], xp),
            lambda: (sm.at[4 * t + 2, pl.ds(na, nb)], fm.at[t, pl.ds(na, nb)], xm),
        )[kind]()
        return pltpu.make_async_remote_copy(
            src_ref=src, dst_ref=dst,
            send_sem=xsem.at[kind, t], recv_sem=xrsem.at[kind, t],
            device_id=peer, device_id_type=MESH,
        )

    def z_move(kind):
        src, dst, peer = (
            lambda: (zz.at[0, pl.ds(0, na)], za, zp),
            lambda: (zz.at[0, pl.ds(na, nb)], zb, zm),
            lambda: (zz.at[1, pl.ds(na, nb)], gp.at[pl.ds(na, nb)], zp),
            lambda: (zz.at[2, pl.ds(0, na)], gm.at[pl.ds(0, na)], zm),
            lambda: (zz.at[1, pl.ds(0, na)], gp.at[pl.ds(0, na)], zp),
            lambda: (zz.at[2, pl.ds(na, nb)], gm.at[pl.ds(na, nb)], zm),
        )[kind]()
        return pltpu.make_async_remote_copy(
            src_ref=src, dst_ref=dst,
            send_sem=zsem.at[kind], recv_sem=zrsem.at[kind],
            device_id=peer, device_id_type=MESH,
        )

    loads[0].wait()

    def wide(v):
        return v.astype(F32)

    def round_trip(t, carry):
        @pl.when(t < 4)
        def _():
            for i in range(4):
                for load in tile_loads(t, i):
                    load.wait()
            tiles = pl.ds(4 * t, 4)

            def tile(n, source):
                cols = pl.ds(pl.multiple_of(n * 256, 256), 256)
                v = nn(source[tiles].reshape(4 * BLK, T), acts[:, cols])
                for i in range(4):
                    for h in range(2):
                        blk[i, 2 * n + h] = v[
                            BLK * i : BLK * i + BLK, BLK * h : BLK * h + BLK
                        ].astype(BF)

            def from_x(n, carry):
                tile(n, xt)
                return carry

            def from_y(n, carry):
                tile(n, yt)
                return carry

            lax.fori_loop(0, 6, from_x, 0)
            lax.fori_loop(6, 9, from_y, 0)
            for i in range(4):
                r = x_of(i) * 4 + z_of(t)
                s = 4 * t + i
                for j in range(cz):
                    b = tbl[r, j]
                    cs[s, j] = blk[i, b, pl.ds(pl.multiple_of(64 * (1 - c), 64), 64), :]
                    sm[s, j] = blk[i, b, pl.ds(pl.multiple_of(64 * c, 64), 64), :]
                core_move(t, i).start()

        @pl.when(t >= 1)
        def _():
            p = t - 1
            x_move(0, p).wait_recv()
            for j in range(na):
                sm[4 * p + 1, j] = (wide(sm[4 * p + 1, j]) + wide(ra[p, j])).astype(BF)
            x_move(4, p).start()
            x_move(1, p).wait_recv()
            for j in range(nb):
                sm[4 * p + 2, na + j] = (
                    wide(sm[4 * p + 2, na + j]) + wide(rb[p, j])
                ).astype(BF)
            x_move(5, p).start()

        @pl.when(t < 4)
        def _():
            for i in range(4):
                s = 4 * t + i
                core_move(t, i).wait_recv()
                for j in range(cz):
                    sm[s, j] = (wide(sm[s, j]) + wide(cr[s, j])).astype(BF)
                if i == 0:
                    x_move(0, t).start()
                    x_move(1, t).start()
                if i == 1:
                    x_move(2, t).start()
                if i == 2:
                    x_move(3, t).start()

        @pl.when((t >= 1) & (t < 4))
        def _():
            p = t - 1
            for kind in (2, 3, 4, 5):
                x_move(kind, p).wait_recv()
            for j in range(cz):
                zz[p, j] = (
                    wide(sm[4 * p + 3, j]) + wide(fp[p, j]) + wide(fm[p, j])
                ).astype(BF)

        @pl.when(t == 1)
        def _():
            z_move(0).start()
            z_move(1).start()

        @pl.when(t == 2)
        def _():
            z_move(2).start()
            z_move(0).wait_recv()
            for j in range(na):
                zz[1, j] = (wide(zz[1, j]) + wide(za[j])).astype(BF)
            z_move(4).start()

        @pl.when(t == 3)
        def _():
            z_move(3).start()
            z_move(1).wait_recv()
            for j in range(nb):
                zz[2, na + j] = (wide(zz[2, na + j]) + wide(zb[j])).astype(BF)
            z_move(5).start()

        return carry

    lax.fori_loop(0, 5, round_trip, 0)

    for load in loads[1:]:
        load.wait()
    for move in r_moves:
        move.wait_recv()
    for e in range(E):
        rem[4 * e : 4 * e + 4, :] = rer[e].astype(F32)
    ret[256:288, :] = rem[...].astype(BF)

    def combine(n, carry):
        cols = pl.ds(pl.multiple_of(n * 512, 512), 512)
        com[:, cols] = nn(wt[...], ret[:, cols]).astype(BF)
        return carry

    lax.fori_loop(0, 4, combine, 0)
    put = pltpu.make_async_copy(com, com_h, lsem.at[4])
    put.start()

    for kind in (2, 3, 4, 5):
        x_move(kind, 3).wait_recv()
        z_move(kind).wait_recv()
    r = x * 4 + z
    for i in range(NB):
        p = tbl[16 + r, i]
        m = tbl[32 + r, i].astype(F32)
        v = wide(sm[15, p]) + wide(fp[3, p]) + wide(fm[3, p]) + wide(gp[p]) + wide(gm[p])
        out = (gg_ref, gu_ref, gd_ref)[i // 6]
        out[:, BLK * (i % 6) : BLK * (i % 6) + BLK] = v * m

    for move in r_moves:
        move.wait_send()

    def drain(t, carry):
        for i in range(4):
            core_move(t, i).wait_send()
        for kind in range(6):
            x_move(kind, t).wait_send()
        return carry

    lax.fori_loop(0, 4, drain, 0)
    for kind in range(6):
        z_move(kind).wait_send()
    put.wait()


def body(tokens, expert_ids, gates, cotangent, gate_weight, up_weight, down_weight, block_masks):
    any_spec = pl.BlockSpec(memory_space=pl.ANY)
    vmem = pl.BlockSpec(memory_space=pltpu.VMEM)
    shape = jax.ShapeDtypeStruct
    dma = pltpu.SemaphoreType.DMA
    xt, yt, acts, rm, rr, wt, tbl, cnt = pl.pallas_call(
        act_kernel,
        out_shape=[
            shape((ROWS, BLK, T), BF),
            shape((ROWS, BLK, T), BF),
            shape((T, 3 * FF), BF),
            shape((256, D), BF),
            shape((E, 4, D), BF),
            shape((T, T), BF),
            shape((48, BLK), jnp.int32),
            shape((8, BLK), F32),
        ],
        in_specs=[any_spec, vmem, vmem] + [any_spec] * 4 + [vmem],
        out_specs=[any_spec] * 6 + [vmem, vmem],
        scratch_shapes=[
            pltpu.VMEM((T, D), BF),
            pltpu.VMEM((T, D), BF),
            pltpu.VMEM((D, FF), BF),
            pltpu.VMEM((D, FF), BF),
            pltpu.VMEM((D, FF), BF),
            pltpu.VMEM((T, T), BF),
            pltpu.VMEM((T, T), BF),
            pltpu.VMEM((256, D), BF),
            pltpu.VMEM((E, 4, D), BF),
            pltpu.VMEM((256, D), BF),
            pltpu.VMEM((E, 4, D), BF),
            pltpu.VMEM((T, D), BF),
            pltpu.VMEM((E, 4, D), BF),
            pltpu.VMEM((T, D), BF),
            pltpu.VMEM((E, 4, D), BF),
            pltpu.VMEM((32, D), F32),
            pltpu.VMEM((T, FF), F32),
            pltpu.VMEM((T, FF), F32),
            pltpu.VMEM((T, 3 * FF), BF),
            pltpu.VMEM((256, D), BF),
            pltpu.VMEM((E, 4, D), BF),
            pltpu.VMEM((ROWS, BLK, T), BF),
            pltpu.VMEM((ROWS, BLK, T), BF),
            pltpu.VMEM((T, T), BF),
            pltpu.VMEM((48, FF), F32),
            pltpu.VMEM((8, BLK), F32),
            pltpu.VMEM((E, 8, BLK), F32),
            dma((9,)),
            dma((6,)),
            dma((5, E)),
            dma((5, E)),
        ],
        compiler_params=pltpu.CompilerParams(collective_id=0, has_side_effects=True),
        name="act",
    )(
        tokens, expert_ids, gates, cotangent,
        gate_weight[0], up_weight[0], down_weight[0], block_masks[0],
    )

    def grads(index, cz):
        na, nb = cz // 2, cz - cz // 2

        def buf(*lead):
            return pltpu.VMEM(lead + (64, BLK), BF)

        return pl.pallas_call(
            functools.partial(grad_kernel, cz),
            out_shape=[
                shape((T, D), BF),
                shape((64, FF), F32),
                shape((64, FF), F32),
                shape((64, FF), F32),
            ],
            in_specs=[any_spec] * 6 + [pl.BlockSpec(memory_space=pltpu.SMEM)],
            out_specs=[any_spec, vmem, vmem, vmem],
            scratch_shapes=[
                pltpu.VMEM((ROWS, BLK, T), BF),
                pltpu.VMEM((ROWS, BLK, T), BF),
                pltpu.VMEM((T, 3 * FF), BF),
                pltpu.VMEM((T, T), BF),
                pltpu.VMEM((T, D), BF),
                pltpu.VMEM((E, 4, D), BF),
                pltpu.VMEM((32, D), F32),
                pltpu.VMEM((T, D), BF),
                pltpu.VMEM((4, NB, BLK, BLK), BF),
                buf(16, cz), buf(16, cz), buf(16, cz),
                buf(4, na), buf(4, nb), buf(4, cz), buf(4, cz),
                buf(3, cz), buf(na), buf(nb), buf(cz), buf(cz),
                dma((5,)),
                dma((2, 16)),
                dma((2, E)),
                dma((2, E)),
                dma((16,)),
                dma((16,)),
                dma((6, 4)),
                dma((6, 4)),
                dma((6,)),
                dma((6,)),
            ],
            compiler_params=pltpu.CompilerParams(
                collective_id=1 + index, has_side_effects=True
            ),
            name=f"grad{cz}",
        )

    most = cnt[0, 0]
    bucket = sum((most > cz).astype(jnp.int32) for cz in BUCKETS[:-1])
    combined, gg, gu, gd = lax.switch(
        bucket,
        [lambda *ops, f=grads(i, cz): tuple(f(*ops)) for i, cz in enumerate(BUCKETS)],
        xt, yt, acts, rm, rr, wt, tbl,
    )
    return (combined, gg[None], gu[None], gd[None])


def solution(mesh):
    return jax.shard_map(
        body,
        mesh=mesh,
        in_specs=(
            P(("dp", "expert"), None),
            P(("dp", "expert"), None),
            P(("dp", "expert"), None),
            P(("dp", "expert"), None),
            P("expert", None, None),
            P("expert", None, None),
            P("expert", None, None),
            P("expert", None, None, None),
        ),
        out_specs=(
            P(("dp", "expert"), None),
            P("expert", "dp", None),
            P("expert", "dp", None),
            P("expert", "dp", None),
        ),
        check_vma=False,
    )
```

time: 441 us -> 106 us (0.24)
  waiting for transfers between devices: 241 us -> 0 us
  Pallas kernels: 0 us -> 92.5 us
  local copies, waits for them, and re-layouts: 75.6 us -> 10.1 us
  matrix products: 47.6 us -> 0 us
  starting transfers between devices: 31 us -> 0 us
  other arithmetic: 28.4 us -> 0 us
  between operations: 14 us -> 2.63 us
    reduce_scatter x3 -> x0, waiting for transfers between devices: 233 us -> none  [the longest x1 96 us: body(): lax.psum_scatter(g_gate.astype(jnp.bfloat16), 'dp', scatter_dimension=1,...]
    pallas_call x0 -> x2, Pallas kernels: none -> 92.5 us  [the longest x1 53.4 us: body(): f(*ops)]
    dot_general x17 -> x0, matrix products: 47.6 us -> none  [the longest x2 9.54 us: body(): jnp.einsum('erd,edf->erf', x_rows, w_up, preferred_element_type=jnp.float32)]
    all_to_all x6 -> x0, starting transfers between devices: 30.4 us -> none  [the longest x2 10.6 us: body(): lax.all_to_all(x_buf, 'expert', split_axis=0, concat_axis=2, tiled=True)]
    broadcast_in_dim x2 -> x0, local copies, waits for them, and re-layouts: 19.8 us -> none  [expand_masks(): jnp.broadcast_to(block_masks.astype(jnp.bfloat16)[:, :, :, None, :, None]...]
    reshape x10 -> x0, local copies, waits for them, and re-layouts: 18.8 us -> none  [the longest x2 4.28 us: body(): dy_buf = dy_buf.reshape(n_expert, local, CAP, width)]
    unnamed x25 -> x13, local copies, waits for them, and re-layouts: 19.9 us -> 8.91 us
    unnamed x4 -> x0, other arithmetic: 10.3 us -> none
  transfers between devices with their start and end apart: 9 -> 0, of which waited for: 6 -> 0; matrix products, arithmetic and copies ran while one was open for 28% -> 0% of each run, Pallas kernels for 0% -> 0%
where the time goes in v1:
time: 106 us; the launch traced here: 105 us
  Pallas kernels  92.5 us (87%)
  local copies, waits for them, and re-layouts  10.1 us (10%)
  between operations  2.63 us (2%)
    pallas_call x1, Pallas kernels, body(): f(*ops)  53.4 us
    pallas_call x1, Pallas kernels, body(): pl.pallas_call(act_kernel, out_shape=[shape((ROWS, BLK, T), BF), shape((R...  39.1 us
    unnamed x13, local copies, waits for them, and re-layouts  8.91 us

profile of v1, /device:TPU:1, one launch (start us, length us, event | category | flops | bytes accessed | tf_op | source)
XLA Modules:
  0.0 105.4 jit_solution(3254353369446779016)
XLA Ops:
  0.6 1.4 %copy.12 = s32[1,3,16,6]{3,2,1,0:T(8,128)} copy(s32[1,3,16,6]{2,0,3,1:T(1,128)} %param.19) | data formatting | bytes 2304 | tf_op args[7]
  2.0 1.5 %copy.13.ids_ref = s32[288,8]{1,0:T(8,128)} copy(s32[288,8]{0,1:T(8,128)} %param.13) | data formatting | bytes 18432 | tf_op args[1]
  3.5 1.5 %copy.14.gat_ref = f32[288,8]{1,0:T(8,128)} copy(f32[288,8]{0,1:T(8,128)} %param.14) | data formatting | bytes 18432 | tf_op args[2]
  5.0 39.1 %act.1 = (bf16[16,128,288]{2,1,0:T(8,128)(2,1)S(1)}, bf16[16,128,288]{2,1,0:T(8,128)(2,1)S(1)}, bf16[288,2304]{1,0:T(8,128)(2,1)}, bf16[256,2048]{1,0:T(8,128)(2...) custom-call(bf16[288,2048]{1,0:T(8,128)(2,1)} %tok_h.1, ...), custom_call_target="tpu_custom_call" | custom-call | tf_op jit(solution)/shard_map/act/pallas_call | solution.py:582
  44.1 1.2 %slice.3 = f32[1,1]{1,0:T(1,128)} slice(f32[8,128]{1,0:T(8,128)} %get-tuple-element.131), slice={[0:1], [0:1]} | slice | bytes 8 | tf_op jit(solution)/shard_map/slice | solution.py:682
  47.3 53.6 %conditional.1 = ((bf16[288,2048]{1,0:T(8,128)(2,1)}, f32[64,768]{1,0:T(8,128)}, f32[64,768]{1,0:T(8,128)}, f32[64,768]{1,0:T(8,128)})) conditional(s32[]{:T(128)} %bitcast.4, (bf16[16,128,288]{2,1,0:T(8,128)(2,1)S(1)}, bf16[16,128,288]{2,1,0:T(8,128)(2,1)S(1)}, bf16[288,2304]{1,0:T(8,128)(2,1)}, ...), branch_computations={%region_0.0_spmd, %region_1.0_spmd, %region_2.0_spmd, %region_3.0_... | conditional | bytes 8 | solution.py:684
  47.3 53.4 %grad13.1 = (bf16[288,2048]{1,0:T(8,128)(2,1)}, f32[64,768]{1,0:T(8,128)}, f32[64,768]{1,0:T(8,128)}, f32[64,768]{1,0:T(8,128)}) custom-call(bf16[16,128,288]{2,1,0:T(8,128)(2,1)S(1)} %get-tuple-element.86.xt_h, bf16[16,128,288]{2,1,0:T(8,128)(2,1)S(1)} %get-tuple-element.87.yt_h, bf16[288,2304]{1,0:T(8,128)(2,1)} %get-tuple-element.88.act_h, ...), custom_call_target="tpu_custom_call" | custom-call | tf_op jit(solution)/shard_map/cond/branch_1_fun/grad13/pallas_call | solution.py:686
  100.9 0.0 copy-start
  100.9 0.0 copy-start.1
  100.9 0.0 copy-start.2
  100.9 2.5 %copy.35 = bf16[288,2048]{1,0:T(8,128)(2,1)} copy(bf16[288,2048]{1,0:T(8,128)(2,1)} %get-tuple-element.168) | data formatting | bytes 2359296
  103.4 0.0 copy-done
  103.4 0.7 copy.36
  104.1 0.0 copy-done.1
  104.1 0.7 copy.37
  104.8 0.0 copy-done.2
  104.8 0.7 copy.38
Async XLA Ops:
  100.9 2.5 %copy-start = (f32[64,768]{1,0:T(8,128)S(1)}, f32[64,768]{1,0:T(8,128)}, u32[]{:S(2)}) copy-start(f32[64,768]{1,0:T(8,128)} %get-tuple-element.142) | copy-start | bytes 589828
  100.9 3.2 %copy-start.1 = (f32[64,768]{1,0:T(8,128)S(1)}, f32[64,768]{1,0:T(8,128)}, u32[]{:S(2)}) copy-start(f32[64,768]{1,0:T(8,128)} %get-tuple-element.141) | copy-start | bytes 589828
  100.9 3.8 %copy-start.2 = (f32[64,768]{1,0:T(8,128)S(1)}, f32[64,768]{1,0:T(8,128)}, u32[]{:S(2)}) copy-start(f32[64,768]{1,0:T(8,128)} %get-tuple-element.140) | copy-start | bytes 589828
